TPU v7x, 32 devices: a whole 2x2x4 slice. The times are simulated.
32 devices in a mesh: view: 4 (over y, x), blk: 8 (over z, core).
Axes of the slice: x: 2, y: 2, z: 4, core: 2. Of those that a mesh axis runs over, the one named last changes fastest.
Arguments:
- estimate: float32 [384, 64, 256], P('blk'), may hold values from 0.5 to 2
- views_seen: float32 [4, 384, 64, 256], P('view', 'blk'), may hold values from 0.2 to 5
- weight_mask: int32 [4, 384, 64, 256], P('view', 'blk'), may hold values from 1 to 3
- psf: float32 [4, 3, 21], P('view'), may hold values from 0.05 to 1
Outputs:
- joined: float32 [384, 64, 256], P('blk')
All inputs are finite; a program needn't handle non-finite values.
Results may differ from a plain program's by a relative error of at most 0.0001.
Values sent between devices are 32-bit elements; how exact they have to be, the bound alone decides.
A program may use at most 128 MiB of HBM per device.

v0:
```python
import jax
import jax.numpy as jnp
from jax import lax
from jax.sharding import PartitionSpec as P

ITERS = 2


def extended(cells, sides, width):
    for axis, dim in sides:
        count = lax.axis_size(axis)
        ends = count - 1
        head = lax.slice_in_dim(cells, 0, width, axis=dim)
        tail = lax.slice_in_dim(cells, cells.shape[dim] - width, cells.shape[dim], axis=dim)
        cells = jnp.concatenate(
            [
                lax.ppermute(tail, axis, [(i, (i + 1) % count) for i in range(ends)]),
                cells,
                lax.ppermute(head, axis, [((i + 1) % count, i) for i in range(ends)]),
            ],
            axis=dim,
        )
    return cells


def band_matrix(kernel, out_count, in_count, offset_by):
    row_index = jnp.arange(out_count)[:, None]
    col_index = jnp.arange(in_count)[None, :]
    offset_table = col_index - row_index + offset_by
    matches = offset_table[:, :, None] == jnp.arange(kernel.shape[0])[None, None, :]
    return jnp.sum(jnp.where(matches, kernel[None, None, :], 0.0), axis=-1)


def sweep_first(padded, kernel, count):
    result = kernel[0] * padded[0:count]
    for tap in range(1, kernel.shape[0]):
        result = result + kernel[tap] * padded[tap : tap + count]
    return result


def sweep_rest(volume, kernel):
    radius = (kernel.shape[-1] - 1) // 2
    along_y = band_matrix(kernel[1], volume.shape[1], volume.shape[1], radius)
    volume = jnp.einsum("ij,xjz->xiz", along_y, volume, precision=lax.Precision.HIGHEST)
    along_z = band_matrix(kernel[2], volume.shape[2], volume.shape[2], radius)
    return jnp.einsum("xyj,kj->xyk", volume, along_z, precision=lax.Precision.HIGHEST)


def body(estimate, views_seen, weight_mask, psf):
    slab = estimate.shape[0]
    radius = (psf.shape[-1] - 1) // 2
    normed = psf / jnp.sum(psf, axis=-1, keepdims=True)
    flipped = normed[:, :, ::-1]
    weights_all = lax.psum(jnp.sum(weight_mask.astype(jnp.float32), axis=0), "view")
    for iteration in range(ITERS):
        padded = extended(estimate, (("blk", 0),), radius)
        forward = normed[0]
        backward = flipped[0]
        blurred = sweep_rest(sweep_first(padded, forward[0], slab), forward)
        quotient = views_seen[0] / blurred
        quotient_wide = extended(quotient, (("blk", 0),), radius)
        correction = sweep_rest(sweep_first(quotient_wide, backward[0], slab), backward)
        numerator = weight_mask[0].astype(jnp.float32) * correction
        summed = lax.psum(numerator, "view")
        estimate = estimate * summed / weights_all
    return estimate


def solution(mesh):
    placed = (
        P("blk", None, None),
        P("view", "blk", None, None),
        P("view", "blk", None, None),
        P("view", None, None),
    )
    return jax.shard_map(
        body, mesh=mesh, in_specs=placed, out_specs=P("blk", None, None), check_vma=False
    )
```

profile of v0, /device:TPU:0, one launch (start us, length us, event | category | flops | bytes accessed | tf_op | source)
XLA Modules:
  0.0 507.7 jit_solution(5480964015441795965)
XLA Ops:
  6.5 0.0 all-reduce.6.cloned.1.call-start
  6.5 2.6 fusion.403
  9.1 3.2 collective-permute-start
  12.3 1.3 collective-permute-start.1
  13.6 0.8 reduce_sum.43
  14.4 0.8 broadcast_divide_fusion
  15.2 0.7 fusion.404
  15.9 0.6 fusion.405
  16.5 0.1 slice.671
  16.6 0.1 slice.672
  16.7 0.2 select_reduce_fusion.2
  17.0 1.0 select_reduce_fusion
  17.9 0.0 copy-start.6
  17.9 0.0 collective-permute-done
  18.0 1.2 constant_dynamic-update-slice_fusion.1
  19.2 0.0 copy-done.1
  19.2 0.5 constant_dynamic-update-slice_fusion
  19.7 0.0 copy-start.7
  19.7 0.0 collective-permute-done.1
  19.7 1.6 constant_dynamic-update-slice_fusion.2
  21.4 0.2 copy-done.7
  21.5 30.9 %fusion.244 = f32[48,256,64]{1,2,0:T(8,128)} fusion(f32[58,64,256]{2,1,0:T(8,128)S(1)} %constant_dynamic-update-slice_fusion.2, f32[58,64,256]{2,1,0:T(8,128)} %copy-done.7, f32[48,64,256]{2,1,0:T(8,128)S(1)} %copy-done.1, f32[]{:T(128)} %bitcast.22, f32[]{:T(128)} %bitcast.21, f32[]{:T(128)} %bitcast.20, f32[]{:T(128)} %bitcast.19, f32[]{:T(128)} %bitcast.18, ...), kind=kOutput, calls=%fused_computation.302 | convolution fusion | flops 636223488 | bytes 69249536 | tf_op jit(solution)/shard_map/ij,xjz->xiz/dot_general | solution.py:44
  52.4 0.0 copy-done.6
  52.4 0.0 copy-start
  52.4 5.9 %bitcast_divide_fusion.1 = f32[48,64,256]{2,1,0:T(8,128)S(1)} fusion(f32[1,48,64,256]{3,2,1,0:T(8,128)} %param.5, f32[48,256,64]{1,2,0:T(8,128)} %fusion.244, f32[256,256]{1,0:T(8,128)S(1)} %get-tuple-element.6), kind=kOutput, calls=%fused_computation.350 | convolution fusion | flops 2416705536 | bytes 9699328 | tf_op jit(solution)/shard_map/xyj,kj->xyk/dot_general | solution.py:46
  58.3 0.0 copy-start.5
  58.3 0.1 fusion.402
  58.4 8.0 %collective-permute-start.2 = (f32[10,64,256]{2,1,0:T(8,128)S(1)}, f32[10,64,256]{2,1,0:T(8,128)S(1)}, u32[]{:S(2)}, u32[]{:S(2)}) collective-permute-start(f32[10,64,256]{2,1,0:T(8,128)S(1)} %get-tuple-element.15), channel_id=1, source_target_pairs={{0,1},{1,2},{2,3},{3,4},{4,5},{5,6},{6,7},{8,9},{9,10},{10,11},{11... | collective-permute-start | bytes 1966088 | tf_op jit(solution)/shard_map/ppermute | solution.py:17
  66.4 1.5 collective-permute-start.3
  67.9 0.0 copy-done
  67.9 2.0 convert_bitcast_fusion
  69.9 0.0 copy-done.5
  69.9 0.0 collective-permute-done.2
  69.9 0.4 collective-permute-done.3
  70.4 0.4 copy-done.9
  70.8 0.8 copy-done.11
  71.6 44.5 %fusion.154 = f32[48,256,64]{1,2,0:T(8,128)} fusion(f32[48,64,256]{2,1,0:T(8,128)} %copy-done.5, f32[10,64,256]{2,1,0:T(8,128)} %copy-done.11, f32[10,64,256]{2,1,0:T(8,128)} %copy-done.9, f32[]{:T(128)} %bitcast.22, f32[]{:T(128)} %bitcast.21, f32[]{:T(128)} %bitcast.20, f32[]{:T(128)} %bitcast.19, f32[]{:T(128)} %bitcast.18, f32[]{:T(128)} %bitcast.17, ...), kind=kOutput, calls=%fused_computation.229 | convolution fusion | flops 651952128 | bytes 7618644 | tf_op jit(solution)/shard_map/ij,xjz->xiz/dot_general | solution.py:44
  116.1 6.2 %fusion.295 = f32[48,64,256]{2,1,0:T(8,128)} fusion(f32[48,256,64]{1,2,0:T(8,128)} %fusion.154, f32[256,256]{1,0:T(8,128)S(1)} %get-tuple-element.5, s32[1,48,64,256]{3,2,1,0:T(8,128)S(1)} %copy-done), kind=kOutput, calls=%fused_computation.358 | convolution fusion | flops 2417491968 | bytes 9699328 | tf_op jit(solution)/shard_map/xyj,kj->xyk/dot_general | solution.py:46
  122.4 0.0 all-reduce.6.cloned.1.call-update
  122.4 0.0 all-reduce.4.cloned.1.call-start
  122.4 146.7 %all-reduce.6.cloned.1.call-done = (f32[48,64,256]{2,1,0:T(8,128)}, f32[48,64,256]{2,1,0:T(8,128)}) async-done(((f32[48,64,256]{2,1,0:T(8,128)}, f32[48,64,256]{2,1,0:T(8,128)}), (f32[48,64,256]{2,1,0:T(8,128)}, f32[48,64,256]{2,1,0:T(8,128)})) %all-reduce.6.cloned.1.call-update) | async-done | bytes 6291472 | tf_op jit(solution)/shard_map/psum | solution.py:54
  269.1 4.7 multiply_divide_fusion.1
  273.8 0.0 copy-start.2
  273.8 1.7 copy-done.2
  275.4 0.1 fusion.401
  275.6 1.8 collective-permute-start.4
  277.4 1.5 collective-permute-start.5
  278.9 0.1 collective-permute-done.4
  279.0 0.8 copy-done.10
  279.9 2.8 collective-permute-done.5
  282.7 45.2 %fusion.79 = f32[48,256,64]{1,2,0:T(8,128)} fusion(f32[48,64,256]{2,1,0:T(8,128)} %copy-done.2, f32[10,64,256]{2,1,0:T(8,128)} %collective-permute-done.5, f32[10,64,256]{2,1,0:T(8,128)} %copy-done.10, f32[]{:T(128)} %bitcast.22, f32[]{:T(128)} %bitcast.21, f32[]{:T(128)} %bitcast.20, f32[]{:T(128)} %bitcast.19, f32[]{:T(128)} %bitcast.18, f32[]{:T(128)} %bitcast.17, ...), kind=kOutput, calls=%fused_computation.172 | convolution fusion | flops 651952128 | bytes 7618644 | tf_op jit(solution)/shard_map/ij,xjz->xiz/dot_general | solution.py:44
  327.9 5.8 %bitcast_divide_fusion = f32[48,64,256]{2,1,0:T(8,128)S(1)} fusion(f32[1,48,64,256]{3,2,1,0:T(8,128)} %param.5, f32[48,256,64]{1,2,0:T(8,128)} %fusion.79, f32[256,256]{1,0:T(8,128)} %copy-done.6), kind=kOutput, calls=%fused_computation.349 | convolution fusion | flops 2416705536 | bytes 9699328 | tf_op jit(solution)/shard_map/xyj,kj->xyk/dot_general | solution.py:46
  333.7 0.0 copy-start.4
  333.7 0.1 fusion.400
  333.8 10.3 %collective-permute-start.6 = (f32[10,64,256]{2,1,0:T(8,128)S(1)}, f32[10,64,256]{2,1,0:T(8,128)S(1)}, u32[]{:S(2)}, u32[]{:S(2)}) collective-permute-start(f32[10,64,256]{2,1,0:T(8,128)S(1)} %get-tuple-element.11), channel_id=1, source_target_pairs={{0,1},{1,2},{2,3},{3,4},{4,5},{5,6},{6,7},{8,9},{9,10},{10,11},{11... | collective-permute-start | bytes 1966088 | tf_op jit(solution)/shard_map/ppermute | solution.py:17
  344.2 1.6 collective-permute-start.7
  345.7 0.1 collective-permute-done.6
  345.8 0.9 copy-done.8
  346.7 1.6 collective-permute-done.7
  348.3 46.7 %fusion.4 = f32[48,256,64]{1,2,0:T(8,128)} fusion(f32[48,64,256]{2,1,0:T(8,128)} %copy-done.4, f32[10,64,256]{2,1,0:T(8,128)} %collective-permute-done.7, f32[10,64,256]{2,1,0:T(8,128)} %copy-done.8, f32[]{:T(128)} %bitcast.22, f32[]{:T(128)} %bitcast.21, f32[]{:T(128)} %bitcast.20, f32[]{:T(128)} %bitcast.19, f32[]{:T(128)} %bitcast.18, f32[]{:T(128)} %bitcast.17, ...), kind=kOutput, calls=%fused_computation.115 | convolution fusion | flops 651952128 | bytes 7618644 | tf_op jit(solution)/shard_map/ij,xjz->xiz/dot_general | solution.py:44
  395.0 6.2 %fusion.298 = f32[48,64,256]{2,1,0:T(8,128)} fusion(f32[48,256,64]{1,2,0:T(8,128)} %fusion.4, f32[256,256]{1,0:T(8,128)S(1)} %get-tuple-element.5, s32[1,48,64,256]{3,2,1,0:T(8,128)S(1)} %copy-done), kind=kOutput, calls=%fused_computation.359 | convolution fusion | flops 2417491968 | bytes 9699328 | tf_op jit(solution)/shard_map/xyj,kj->xyk/dot_general | solution.py:46
  401.2 0.0 all-reduce.4.cloned.1.call-update
  401.2 94.0 %all-reduce.4.cloned.1.call-done = f32[48,64,256]{2,1,0:T(8,128)} async-done(((f32[48,64,256]{2,1,0:T(8,128)}), f32[48,64,256]{2,1,0:T(8,128)}) %all-reduce.4.cloned.1.call-update) | async-done | bytes 3145744 | tf_op jit(solution)/shard_map/psum | solution.py:64
  495.2 5.7 %multiply_divide_fusion = f32[48,64,256]{2,1,0:T(8,128)} fusion(f32[48,64,256]{2,1,0:T(8,128)} %get-tuple-element.9, f32[48,64,256]{2,1,0:T(8,128)S(1)} %copy-done.3, f32[48,64,256]{2,1,0:T(8,128)} %all-reduce.4.cloned.1.call-done), kind=kLoop, calls=%fused_computation.351 | loop fusion | flops 1572864 | bytes 12582912 | tf_op jit(solution)/shard_map/div | solution.py:65
  (11 shorter events, 0.1 us)
Async XLA Ops:
  6.5 12.7 %copy-start.1 = (f32[48,64,256]{2,1,0:T(8,128)S(1)}, f32[48,64,256]{2,1,0:T(8,128)}, u32[]{:S(2)}) copy-start(f32[48,64,256]{2,1,0:T(8,128)} %param.4) | copy-start | bytes 9437188
  6.5 262.6 %all-reduce.6.cloned.1.call-start = ((), (), s32[]{:S(2)}) async-start(), calls=%async_computation.1 | async-start | bytes 12582912 | tf_op jit(solution)/shard_map/psum | solution.py:54
  9.1 8.8 %collective-permute-start = (f32[10,64,256]{2,1,0:T(8,128)}, f32[10,64,256]{2,1,0:T(8,128)}, u32[]{:S(2)}, u32[]{:S(2)}) collective-permute-start(f32[10,64,256]{2,1,0:T(8,128)} %get-tuple-element.19), channel_id=1, source_target_pairs={{0,1},{1,2},{2,3},{3,4},{4,5},{5,6},{6,7},{8,9},{9,10},{10,11},{11... | collective-permute-start | bytes 1966088 | tf_op jit(solution)/shard_map/ppermute | solution.py:17
  12.3 7.4 %collective-permute-start.1 = (f32[10,64,256]{2,1,0:T(8,128)}, f32[10,64,256]{2,1,0:T(8,128)}, u32[]{:S(2)}, u32[]{:S(2)}) collective-permute-start(f32[10,64,256]{2,1,0:T(8,128)} %get-tuple-element.20), channel_id=1, source_target_pairs={{1,0},{2,1},{3,2},{4,3},{5,4},{6,5},{7,6},{9,8},{10,9},{11,10},{12... | collective-permute-start | bytes 1966088 | tf_op jit(solution)/shard_map/ppermute | solution.py:19
  17.9 34.5 %copy-start.6 = (f32[256,256]{1,0:T(8,128)}, f32[256,256]{1,0:T(8,128)S(1)}, u32[]{:S(2)}) copy-start(f32[256,256]{1,0:T(8,128)S(1)} %get-tuple-element.6) | copy-start | bytes 786436
  19.7 1.8 copy-start.7
  52.4 15.4 %copy-start = (s32[1,48,64,256]{3,2,1,0:T(8,128)S(1)}, s32[1,48,64,256]{3,2,1,0:T(8,128)}, u32[]{:S(2)}) copy-start(s32[1,48,64,256]{3,2,1,0:T(8,128)} %param.6) | copy-start | bytes 9437188
  58.3 11.6 %copy-start.5 = (f32[48,64,256]{2,1,0:T(8,128)}, f32[48,64,256]{2,1,0:T(8,128)S(1)}, u32[]{:S(2)}) copy-start(f32[48,64,256]{2,1,0:T(8,128)S(1)} %bitcast_divide_fusion.1) | copy-start | bytes 9437188
  58.4 11.5 %collective-permute-start.2 = (f32[10,64,256]{2,1,0:T(8,128)S(1)}, f32[10,64,256]{2,1,0:T(8,128)S(1)}, u32[]{:S(2)}, u32[]{:S(2)}) collective-permute-start(f32[10,64,256]{2,1,0:T(8,128)S(1)} %get-tuple-element.15), channel_id=1, source_target_pairs={{0,1},{1,2},{2,3},{3,4},{4,5},{5,6},{6,7},{8,9},{9,10},{10,11},{11... | collective-permute-start | bytes 1966088 | tf_op jit(solution)/shard_map/ppermute | solution.py:17
  66.4 4.0 collective-permute-start.3
  69.9 0.8 copy-start.9
  70.7 0.8 copy-start.11
  122.4 372.8 %all-reduce.4.cloned.1.call-start = ((), (), s32[]{:S(2)}) async-start(), calls=%async_computation | async-start | bytes 6291456 | tf_op jit(solution)/shard_map/psum | solution.py:64
  273.8 1.7 copy-start.2
  275.6 3.5 collective-permute-start.4
  277.4 5.3 %collective-permute-start.5 = (f32[10,64,256]{2,1,0:T(8,128)S(1)}, f32[10,64,256]{2,1,0:T(8,128)}, u32[]{:S(2)}, u32[]{:S(2)}) collective-permute-start(f32[10,64,256]{2,1,0:T(8,128)S(1)} %get-tuple-element.14), channel_id=1, source_target_pairs={{1,0},{2,1},{3,2},{4,3},{5,4},{6,5},{7,6},{9,8},{10,9},{11,10},{12... | collective-permute-start | bytes 1966088 | tf_op jit(solution)/shard_map/ppermute | solution.py:19
  279.0 0.8 copy-start.10
  333.7 12.1 %copy-start.4 = (f32[48,64,256]{2,1,0:T(8,128)}, f32[48,64,256]{2,1,0:T(8,128)S(1)}, u32[]{:S(2)}) copy-start(f32[48,64,256]{2,1,0:T(8,128)S(1)} %bitcast_divide_fusion) | copy-start | bytes 9437188
  333.8 12.0 %collective-permute-start.6 = (f32[10,64,256]{2,1,0:T(8,128)S(1)}, f32[10,64,256]{2,1,0:T(8,128)S(1)}, u32[]{:S(2)}, u32[]{:S(2)}) collective-permute-start(f32[10,64,256]{2,1,0:T(8,128)S(1)} %get-tuple-element.11), channel_id=1, source_target_pairs={{0,1},{1,2},{2,3},{3,4},{4,5},{5,6},{6,7},{8,9},{9,10},{10,11},{11... | collective-permute-start | bytes 1966088 | tf_op jit(solution)/shard_map/ppermute | solution.py:17
  344.2 4.1 collective-permute-start.7
  345.8 0.9 copy-start.8
  401.2 94.0 %copy-start.3 = (f32[48,64,256]{2,1,0:T(8,128)S(1)}, f32[48,64,256]{2,1,0:T(8,128)}, u32[]{:S(2)}) copy-start(f32[48,64,256]{2,1,0:T(8,128)} %copy-done.2) | copy-start | bytes 9437188
Sparse Core Ops, SparseCore 0:
  122.5 146.5 all-reduce.5
  401.3 93.7 all-reduce.3
where the time goes:
time: 509 us; the launch traced here: 508 us
  waiting for transfers between devices  246 us (48%)
  matrix products  191 us (38%)
  starting transfers between devices  29.1 us (6%)
  other arithmetic  15.2 us (3%)
  between operations  13.7 us (3%)
  local copies, waits for them, and re-layouts  12.6 us (2%)
    dot_general x4, matrix products, sweep_rest(): jnp.einsum('ij,xjz->xiz', along_y, volume, precision=lax.Precision.HIGHEST)  167 us
    psum x1, waiting for transfers between devices, body(): lax.psum(jnp.sum(weight_mask.astype(jnp.float32), axis=0), 'view')  147 us
    psum x1, waiting for transfers between devices, body(): summed = lax.psum(numerator, 'view')  94 us
    dot_general x4, matrix products, sweep_rest(): jnp.einsum('xyj,kj->xyk', volume, along_z, precision=lax.Precision.HIGHEST)  24.1 us
    ppermute x4, starting transfers between devices, extended(): lax.ppermute(tail, axis, [(i, (i + 1) % count) for i in range(ends)])  23.3 us
    div x2, other arithmetic, body(): estimate = estimate * summed / weights_all  10.4 us
  transfers between devices with their start and end apart: 10, of which 7 were waited for; matrix products, arithmetic and copies ran while one was open for 2% of the time, Pallas kernels for 0%

commit v1 on v0

--- a/solution.py
+++ b/solution.py
@@ -51,7 +51,9 @@
     radius = (psf.shape[-1] - 1) // 2
     normed = psf / jnp.sum(psf, axis=-1, keepdims=True)
     flipped = normed[:, :, ::-1]
-    weights_all = lax.psum(jnp.sum(weight_mask.astype(jnp.float32), axis=0), "view")
+    weights_all = jnp.sum(
+        lax.all_gather(jnp.sum(weight_mask.astype(jnp.float32), axis=0), "view"), axis=0
+    )
     for iteration in range(ITERS):
         padded = extended(estimate, (("blk", 0),), radius)
         forward = normed[0]

time: 509 us -> 466 us (0.916)
  waiting for transfers between devices: 246 us -> 189 us
  other arithmetic: 15.2 us -> 23.6 us
    psum x1 -> x0, waiting for transfers between devices: 147 us -> none  [body(): lax.psum(jnp.sum(weight_mask.astype(jnp.float32), axis=0), 'view')]
    psum x1 -> x2, waiting for transfers between devices: 94 us -> 179 us  [body(): summed = lax.psum(numerator, 'view')]
    all_gather x0 -> x1, waiting for transfers between devices: none -> 8.52 us  [body(): lax.all_gather(jnp.sum(weight_mask.astype(jnp.float32), axis=0), 'view')]
    reduce_sum x0 -> x1, other arithmetic: none -> 7.95 us  [body(): jnp.sum(lax.all_gather(jnp.sum(weight_mask.astype(jnp.float32), axis=0),...]
  transfers between devices with their start and end apart: 10 -> 11, of which waited for: 7 -> 6; matrix products, arithmetic and copies ran while one was open for 2% -> 22% of each run, Pallas kernels for 0% -> 0%
where the time goes in v1:
time: 466 us; the launch traced here: 464 us
  matrix products  193 us (41%)
  waiting for transfers between devices  189 us (41%)
  starting transfers between devices  32.8 us (7%)
  other arithmetic  23.6 us (5%)
  between operations  13.3 us (3%)
  local copies, waits for them, and re-layouts  12.8 us (3%)
    psum x2, waiting for transfers between devices, body(): summed = lax.psum(numerator, 'view')  179 us
    dot_general x4, matrix products, sweep_rest(): jnp.einsum('ij,xjz->xiz', along_y, volume, precision=lax.Precision.HIGHEST)  169 us
    ppermute x4, starting transfers between devices, extended(): lax.ppermute(tail, axis, [(i, (i + 1) % count) for i in range(ends)])  27.6 us
    dot_general x4, matrix products, sweep_rest(): jnp.einsum('xyj,kj->xyk', volume, along_z, precision=lax.Precision.HIGHEST)  23.9 us
    div x2, other arithmetic, body(): estimate = estimate * summed / weights_all  10.4 us
  transfers between devices with their start and end apart: 11, of which 6 were waited for; matrix products, arithmetic and copies ran while one was open for 22% of the time, Pallas kernels for 0%

profile of v1, /device:TPU:0, one launch (start us, length us, event | category | flops | bytes accessed | tf_op | source)
XLA Modules:
  0.0 464.4 jit_solution(2979616020431682387)
XLA Ops:
  6.5 0.0 all-gather.2.cloned.1.call-start
  6.5 3.9 convert_element_type.8
  10.5 0.0 all-gather.2.cloned.1.call-update
  10.5 0.0 all-reduce.3.cloned.1.call-start
  10.5 1.8 copy-done.2
  12.4 1.2 fusion.401
  13.6 3.2 collective-permute-start
  16.8 1.3 collective-permute-start.1
  18.1 0.0 copy-done.8
  18.1 0.1 reduce_sum.51
  18.2 0.1 broadcast_divide_fusion
  18.3 0.7 fusion.402
  19.0 0.6 fusion.403
  19.6 0.1 slice.671
  19.7 0.1 slice.672
  19.8 0.2 select_reduce_fusion.2
  20.0 1.0 select_reduce_fusion
  21.0 0.0 copy-start.6
  21.0 0.0 collective-permute-done
  21.0 1.4 constant_dynamic-update-slice_fusion.1
  22.4 0.5 constant_dynamic-update-slice_fusion
  22.9 0.0 copy-start.7
  22.9 0.0 collective-permute-done.1
  22.9 1.7 constant_dynamic-update-slice_fusion.2
  24.7 0.1 copy-done.7
  24.7 30.9 %fusion.244 = f32[48,256,64]{1,2,0:T(8,128)} fusion(f32[58,64,256]{2,1,0:T(8,128)S(1)} %constant_dynamic-update-slice_fusion.2, f32[58,64,256]{2,1,0:T(8,128)} %copy-done.7, f32[48,64,256]{2,1,0:T(8,128)S(1)} %copy-done.2, f32[]{:T(128)} %bitcast.22, f32[]{:T(128)} %bitcast.21, f32[]{:T(128)} %bitcast.20, f32[]{:T(128)} %bitcast.19, f32[]{:T(128)} %bitcast.18, ...), kind=kOutput, calls=%fused_computation.302 | convolution fusion | flops 636223488 | bytes 69249536 | tf_op jit(solution)/shard_map/ij,xjz->xiz/dot_general | solution.py:44
  55.6 0.0 copy-done.6
  55.6 5.7 %bitcast_divide_fusion.1 = f32[48,64,256]{2,1,0:T(8,128)S(1)} fusion(f32[1,48,64,256]{3,2,1,0:T(8,128)} %param.5, f32[48,256,64]{1,2,0:T(8,128)} %fusion.244, f32[256,256]{1,0:T(8,128)S(1)} %get-tuple-element.6), kind=kOutput, calls=%fused_computation.350 | convolution fusion | flops 2416705536 | bytes 9699328 | tf_op jit(solution)/shard_map/xyj,kj->xyk/dot_general | solution.py:46
  61.4 0.1 fusion.400
  61.4 1.3 collective-permute-start.3
  62.7 10.3 %collective-permute-start.2 = (f32[10,64,256]{2,1,0:T(8,128)S(1)}, f32[10,64,256]{2,1,0:T(8,128)S(1)}, u32[]{:S(2)}, u32[]{:S(2)}) collective-permute-start(f32[10,64,256]{2,1,0:T(8,128)S(1)} %get-tuple-element.13), channel_id=1, source_target_pairs={{0,1},{1,2},{2,3},{3,4},{4,5},{5,6},{6,7},{8,9},{9,10},{10,11},{11... | collective-permute-start | bytes 1966088 | tf_op jit(solution)/shard_map/ppermute | solution.py:17
  73.1 0.0 collective-permute-done.3
  73.1 1.5 collective-permute-done.2
  74.5 0.0 copy-done.5
  74.6 0.8 copy-done.12
  75.4 45.7 %fusion.154 = f32[48,256,64]{1,2,0:T(8,128)} fusion(f32[48,64,256]{2,1,0:T(8,128)} %copy-done.5, f32[10,64,256]{2,1,0:T(8,128)} %copy-done.10, f32[10,64,256]{2,1,0:T(8,128)} %copy-done.12, f32[]{:T(128)} %bitcast.22, f32[]{:T(128)} %bitcast.21, f32[]{:T(128)} %bitcast.20, f32[]{:T(128)} %bitcast.19, f32[]{:T(128)} %bitcast.18, f32[]{:T(128)} %bitcast.17, ...), kind=kOutput, calls=%fused_computation.229 | convolution fusion | flops 651952128 | bytes 7618644 | tf_op jit(solution)/shard_map/ij,xjz->xiz/dot_general | solution.py:44
  121.1 6.2 %bitcast_multiply_fusion.1 = f32[48,64,256]{2,1,0:T(8,128)} fusion(f32[48,256,64]{1,2,0:T(8,128)} %fusion.154, f32[256,256]{1,0:T(8,128)S(1)} %get-tuple-element.5, s32[1,48,64,256]{3,2,1,0:T(8,128)S(1)} %copy-done), kind=kOutput, calls=%fused_computation.352 | convolution fusion | flops 2417491968 | bytes 9699328 | tf_op jit(solution)/shard_map/xyj,kj->xyk/dot_general | solution.py:46
  127.3 0.0 all-reduce.3.cloned.1.call-update
  127.3 0.0 all-reduce.5.cloned.1.call-start
  127.3 8.5 %all-gather.2.cloned.1.call-done = f32[4,48,64,256]{3,2,1,0:T(8,128)} async-done(((f32[1,48,64,256]{3,2,1,0:T(8,128)}), f32[4,48,64,256]{3,2,1,0:T(8,128)}) %all-gather.2.cloned.1.call-update) | async-done | bytes 12582928 | tf_op jit(solution)/shard_map/all_gather | solution.py:55
  135.9 8.0 %reduce_sum.62 = f32[48,64,256]{2,1,0:T(8,128)} reduce(f32[4,48,64,256]{3,2,1,0:T(8,128)} %all-gather.2.cloned.1.call-done, f32[]{:T(128)} %constant.2.clone.1), dimensions={0}, to_apply=%region_6.7 | reduce | flops 2359296 | bytes 15728644 | tf_op jit(solution)/shard_map/reduce_sum | solution.py:54
  143.8 82.4 %all-reduce.3.cloned.1.call-done = f32[48,64,256]{2,1,0:T(8,128)} async-done(((f32[48,64,256]{2,1,0:T(8,128)}), f32[48,64,256]{2,1,0:T(8,128)}) %all-reduce.3.cloned.1.call-update) | async-done | bytes 3145744 | tf_op jit(solution)/shard_map/psum | solution.py:66
  226.2 4.7 %multiply_divide_fusion.1 = f32[48,64,256]{2,1,0:T(8,128)S(1)} fusion(f32[48,64,256]{2,1,0:T(8,128)} %reduce_sum.62, f32[48,64,256]{2,1,0:T(8,128)} %param.4, f32[48,64,256]{2,1,0:T(8,128)} %all-reduce.3.cloned.1.call-done), kind=kLoop, calls=%fused_computation.356 | loop fusion | flops 1572864 | bytes 12582912 | tf_op jit(solution)/shard_map/div | solution.py:67
  230.9 1.6 copy-done.3
  232.5 0.1 fusion.399
  232.7 1.3 collective-permute-start.5
  234.0 3.9 collective-permute-start.4
  237.8 0.0 collective-permute-done.5
  237.8 0.9 copy-done.11
  238.7 0.1 collective-permute-done.4
  238.8 45.3 %fusion.79 = f32[48,256,64]{1,2,0:T(8,128)} fusion(f32[48,64,256]{2,1,0:T(8,128)} %copy-done.3, f32[10,64,256]{2,1,0:T(8,128)} %copy-done.11, f32[10,64,256]{2,1,0:T(8,128)} %collective-permute-done.4, f32[]{:T(128)} %bitcast.22, f32[]{:T(128)} %bitcast.21, f32[]{:T(128)} %bitcast.20, f32[]{:T(128)} %bitcast.19, f32[]{:T(128)} %bitcast.18, f32[]{:T(128)} %bitcast.17, ...), kind=kOutput, calls=%fused_computation.172 | convolution fusion | flops 651952128 | bytes 7618644 | tf_op jit(solution)/shard_map/ij,xjz->xiz/dot_general | solution.py:44
  284.1 5.8 %bitcast_divide_fusion = f32[48,64,256]{2,1,0:T(8,128)S(1)} fusion(f32[1,48,64,256]{3,2,1,0:T(8,128)} %param.5, f32[48,256,64]{1,2,0:T(8,128)} %fusion.79, f32[256,256]{1,0:T(8,128)} %copy-done.6), kind=kOutput, calls=%fused_computation.349 | convolution fusion | flops 2416705536 | bytes 9699328 | tf_op jit(solution)/shard_map/xyj,kj->xyk/dot_general | solution.py:46
  290.0 0.0 copy-start.4
  290.0 0.1 fusion.398
  290.1 1.3 collective-permute-start.7
  291.4 10.2 %collective-permute-start.6 = (f32[10,64,256]{2,1,0:T(8,128)S(1)}, f32[10,64,256]{2,1,0:T(8,128)}, u32[]{:S(2)}, u32[]{:S(2)}) collective-permute-start(f32[10,64,256]{2,1,0:T(8,128)S(1)} %get-tuple-element.9), channel_id=1, source_target_pairs={{0,1},{1,2},{2,3},{3,4},{4,5},{5,6},{6,7},{8,9},{9,10},{10,11},{11... | collective-permute-start | bytes 1966088 | tf_op jit(solution)/shard_map/ppermute | solution.py:17
  301.6 0.0 collective-permute-done.7
  301.6 0.8 copy-done.9
  302.4 0.1 collective-permute-done.6
  302.5 46.7 %fusion.4 = f32[48,256,64]{1,2,0:T(8,128)} fusion(f32[48,64,256]{2,1,0:T(8,128)} %copy-done.4, f32[10,64,256]{2,1,0:T(8,128)} %copy-done.9, f32[10,64,256]{2,1,0:T(8,128)} %collective-permute-done.6, f32[]{:T(128)} %bitcast.22, f32[]{:T(128)} %bitcast.21, f32[]{:T(128)} %bitcast.20, f32[]{:T(128)} %bitcast.19, f32[]{:T(128)} %bitcast.18, f32[]{:T(128)} %bitcast.17, ...), kind=kOutput, calls=%fused_computation.115 | convolution fusion | flops 651952128 | bytes 7618644 | tf_op jit(solution)/shard_map/ij,xjz->xiz/dot_general | solution.py:44
  349.3 6.2 %bitcast_multiply_fusion = f32[48,64,256]{2,1,0:T(8,128)} fusion(f32[48,256,64]{1,2,0:T(8,128)} %fusion.4, f32[256,256]{1,0:T(8,128)S(1)} %get-tuple-element.5, s32[1,48,64,256]{3,2,1,0:T(8,128)S(1)} %copy-done), kind=kOutput, calls=%fused_computation.351 | convolution fusion | flops 2417491968 | bytes 9699328 | tf_op jit(solution)/shard_map/xyj,kj->xyk/dot_general | solution.py:46
  355.5 0.0 all-reduce.5.cloned.1.call-update
  355.5 96.6 %all-reduce.5.cloned.1.call-done = f32[48,64,256]{2,1,0:T(8,128)} async-done(((f32[48,64,256]{2,1,0:T(8,128)}), f32[48,64,256]{2,1,0:T(8,128)}) %all-reduce.5.cloned.1.call-update) | async-done | bytes 3145744 | tf_op jit(solution)/shard_map/psum | solution.py:66
  452.1 5.7 %multiply_divide_fusion = f32[48,64,256]{2,1,0:T(8,128)} fusion(f32[48,64,256]{2,1,0:T(8,128)S(1)} %copy-done.1, f32[48,64,256]{2,1,0:T(8,128)} %copy-done.3, f32[48,64,256]{2,1,0:T(8,128)} %all-reduce.5.cloned.1.call-done), kind=kLoop, calls=%fused_computation.353 | loop fusion | flops 1572864 | bytes 12582912 | tf_op jit(solution)/shard_map/div | solution.py:67
  (17 shorter events, 0.1 us)
Async XLA Ops:
  6.5 129.3 %all-gather.2.cloned.1.call-start = ((), (), s32[]{:S(2)}) async-start(), calls=%async_computation.1 | async-start | bytes 15728640 | tf_op jit(solution)/shard_map/all_gather | solution.py:55
  10.5 1.9 copy-start.2
  10.5 7.6 %copy-start.8 = (f32[1,3,21]{2,0,1:T(1,128)S(1)}, f32[1,3,21]{2,0,1:T(1,128)}, u32[]{:S(2)}) copy-start(f32[1,3,21]{2,0,1:T(1,128)} %param.7) | copy-start | bytes 760
  10.5 215.7 %all-reduce.3.cloned.1.call-start = ((), (), s32[]{:S(2)}) async-start(), calls=%async_computation | async-start | bytes 6291456 | tf_op jit(solution)/shard_map/psum | solution.py:66
  13.6 7.4 %collective-permute-start = (f32[10,64,256]{2,1,0:T(8,128)}, f32[10,64,256]{2,1,0:T(8,128)}, u32[]{:S(2)}, u32[]{:S(2)}) collective-permute-start(f32[10,64,256]{2,1,0:T(8,128)} %get-tuple-element.17), channel_id=1, source_target_pairs={{0,1},{1,2},{2,3},{3,4},{4,5},{5,6},{6,7},{8,9},{9,10},{10,11},{11... | collective-permute-start | bytes 1966088 | tf_op jit(solution)/shard_map/ppermute | solution.py:17
  16.8 6.2 %collective-permute-start.1 = (f32[10,64,256]{2,1,0:T(8,128)}, f32[10,64,256]{2,1,0:T(8,128)}, u32[]{:S(2)}, u32[]{:S(2)}) collective-permute-start(f32[10,64,256]{2,1,0:T(8,128)} %get-tuple-element.18), channel_id=1, source_target_pairs={{1,0},{2,1},{3,2},{4,3},{5,4},{6,5},{7,6},{9,8},{10,9},{11,10},{12... | collective-permute-start | bytes 1966088 | tf_op jit(solution)/shard_map/ppermute | solution.py:19
  21.0 34.6 %copy-start.6 = (f32[256,256]{1,0:T(8,128)}, f32[256,256]{1,0:T(8,128)S(1)}, u32[]{:S(2)}) copy-start(f32[256,256]{1,0:T(8,128)S(1)} %get-tuple-element.6) | copy-start | bytes 786436
  22.9 1.8 copy-start.7
  61.3 13.2 %copy-start.5 = (f32[48,64,256]{2,1,0:T(8,128)}, f32[48,64,256]{2,1,0:T(8,128)S(1)}, u32[]{:S(2)}) copy-start(f32[48,64,256]{2,1,0:T(8,128)S(1)} %bitcast_divide_fusion.1) | copy-start | bytes 9437188
  61.4 11.6 %collective-permute-start.3 = (f32[10,64,256]{2,1,0:T(8,128)S(1)}, f32[10,64,256]{2,1,0:T(8,128)S(1)}, u32[]{:S(2)}, u32[]{:S(2)}) collective-permute-start(f32[10,64,256]{2,1,0:T(8,128)S(1)} %get-tuple-element.14), channel_id=1, source_target_pairs={{1,0},{2,1},{3,2},{4,3},{5,4},{6,5},{7,6},{9,8},{10,9},{11,10},{12... | collective-permute-start | bytes 1966088 | tf_op jit(solution)/shard_map/ppermute | solution.py:19
  62.7 11.8 %collective-permute-start.2 = (f32[10,64,256]{2,1,0:T(8,128)S(1)}, f32[10,64,256]{2,1,0:T(8,128)S(1)}, u32[]{:S(2)}, u32[]{:S(2)}) collective-permute-start(f32[10,64,256]{2,1,0:T(8,128)S(1)} %get-tuple-element.13), channel_id=1, source_target_pairs={{0,1},{1,2},{2,3},{3,4},{4,5},{5,6},{6,7},{8,9},{9,10},{10,11},{11... | collective-permute-start | bytes 1966088 | tf_op jit(solution)/shard_map/ppermute | solution.py:17
  73.1 1.5 copy-start.10
  74.6 0.8 copy-start.12
  75.4 45.7 %copy-start = (s32[1,48,64,256]{3,2,1,0:T(8,128)S(1)}, s32[1,48,64,256]{3,2,1,0:T(8,128)}, u32[]{:S(2)}) copy-start(s32[1,48,64,256]{3,2,1,0:T(8,128)} %param.6) | copy-start | bytes 9437188
  127.3 324.8 %all-reduce.5.cloned.1.call-start = ((), (), s32[]{:S(2)}) async-start(), calls=%async_computation.2 | async-start | bytes 6291456 | tf_op jit(solution)/shard_map/psum | solution.py:66
  230.9 1.7 copy-start.3
  232.7 5.2 %collective-permute-start.5 = (f32[10,64,256]{2,1,0:T(8,128)S(1)}, f32[10,64,256]{2,1,0:T(8,128)S(1)}, u32[]{:S(2)}, u32[]{:S(2)}) collective-permute-start(f32[10,64,256]{2,1,0:T(8,128)S(1)} %get-tuple-element.12), channel_id=1, source_target_pairs={{1,0},{2,1},{3,2},{4,3},{5,4},{6,5},{7,6},{9,8},{10,9},{11,10},{12... | collective-permute-start | bytes 1966088 | tf_op jit(solution)/shard_map/ppermute | solution.py:19
  234.0 4.9 %collective-permute-start.4 = (f32[10,64,256]{2,1,0:T(8,128)S(1)}, f32[10,64,256]{2,1,0:T(8,128)}, u32[]{:S(2)}, u32[]{:S(2)}) collective-permute-start(f32[10,64,256]{2,1,0:T(8,128)S(1)} %get-tuple-element.11), channel_id=1, source_target_pairs={{0,1},{1,2},{2,3},{3,4},{4,5},{5,6},{6,7},{8,9},{9,10},{10,11},{11... | collective-permute-start | bytes 1966088 | tf_op jit(solution)/shard_map/ppermute | solution.py:17
  237.8 0.9 copy-start.11
  290.0 11.6 %copy-start.4 = (f32[48,64,256]{2,1,0:T(8,128)}, f32[48,64,256]{2,1,0:T(8,128)S(1)}, u32[]{:S(2)}) copy-start(f32[48,64,256]{2,1,0:T(8,128)S(1)} %bitcast_divide_fusion) | copy-start | bytes 9437188
  290.1 11.5 %collective-permute-start.7 = (f32[10,64,256]{2,1,0:T(8,128)S(1)}, f32[10,64,256]{2,1,0:T(8,128)S(1)}, u32[]{:S(2)}, u32[]{:S(2)}) collective-permute-start(f32[10,64,256]{2,1,0:T(8,128)S(1)} %get-tuple-element.10), channel_id=1, source_target_pairs={{1,0},{2,1},{3,2},{4,3},{5,4},{6,5},{7,6},{9,8},{10,9},{11,10},{12... | collective-permute-start | bytes 1966088 | tf_op jit(solution)/shard_map/ppermute | solution.py:19
  291.4 11.2 %collective-permute-start.6 = (f32[10,64,256]{2,1,0:T(8,128)S(1)}, f32[10,64,256]{2,1,0:T(8,128)}, u32[]{:S(2)}, u32[]{:S(2)}) collective-permute-start(f32[10,64,256]{2,1,0:T(8,128)S(1)} %get-tuple-element.9), channel_id=1, source_target_pairs={{0,1},{1,2},{2,3},{3,4},{4,5},{5,6},{6,7},{8,9},{9,10},{10,11},{11... | collective-permute-start | bytes 1966088 | tf_op jit(solution)/shard_map/ppermute | solution.py:17
  301.6 0.8 copy-start.9
  355.5 96.6 %copy-start.1 = (f32[48,64,256]{2,1,0:T(8,128)S(1)}, f32[48,64,256]{2,1,0:T(8,128)}, u32[]{:S(2)}) copy-start(f32[48,64,256]{2,1,0:T(8,128)} %reduce_sum.62) | copy-start | bytes 9437188
Sparse Core Ops, SparseCore 0:
  10.6 125.2 all-gather.1
  139.0 87.2 all-reduce.2
  355.6 96.4 all-reduce.4
